TPU v7x, 32 devices: a whole 2x2x4 slice. The times are simulated.
32 devices in a mesh: lon: 2 (over x), lat: 4 (over y, core), lev: 4 (over z).
Axes of the slice: x: 2, y: 2, z: 4, core: 2. Of those that a mesh axis runs over, the one named last changes fastest.
Arguments:
- fields: float32 [3, 8, 60, 512], P(None, 'lev', 'lon', 'lat'), may hold values from -6 to 6
- spectral_coeffs: float32 [3, 8], P(None, 'lev'), may hold values from 0.3 to 3
- mlp_in: bfloat16 [384, 24], replicated, may hold values from -1.25 to 1.25
- mlp_mid: bfloat16 [2, 384, 384], replicated, may hold values from -0.3125 to 0.3125
- mlp_out: bfloat16 [24, 384], replicated, may hold values from -0.3125 to 0.3125
Outputs:
- updated: float32 [3, 8, 60, 512], P(None, 'lev', 'lon', 'lat')
All inputs are finite; a program needn't handle non-finite values.
Results may differ from a plain program's by a relative error of at most 0.0012.
Values may be sent and summed in bfloat16 or wider, within the bound.
No kernel may reach another device: no remote copies, remote signals or barrier semaphores. Data moves between devices by JAX's collectives and lax.ppermute only.
A program may use at most 64 MiB of HBM per device.

v0:
```python
import functools

import jax
import jax.numpy as jnp
import numpy as np
from jax import lax
from jax.experimental import pallas as pl
from jax.experimental.pallas import tpu as pltpu
from jax.sharding import PartitionSpec as P


WAVES = 320
KMAX = 320
SUBSTEPS = 2


highest = lax.Precision.HIGHEST
LANES = 128
GROUP = 2048
PLANE_LIMIT = 4 * 1024 * 1024


def round_up(value, unit):
    return -(-value // unit) * unit


def forward_table(lon_ids, total_lon, waves):
    wave_ids = jnp.arange(waves, dtype=jnp.int32)
    phase = (lon_ids[:, None] * wave_ids[None, :] % total_lon).astype(jnp.float32) * (
        2.0 * jnp.pi / total_lon
    )
    return jnp.concatenate([jnp.cos(phase), -jnp.sin(phase)], axis=1) / total_lon


def inverse_table(lon_ids, total_lon, waves):
    wave_ids = jnp.arange(waves, dtype=jnp.int32)
    phase = (wave_ids[:, None] * lon_ids[None, :] % total_lon).astype(jnp.float32) * (
        2.0 * jnp.pi / total_lon
    )
    weight = jnp.where(wave_ids == 0, 1.0, 2.0).astype(jnp.float32)[:, None]
    return jnp.concatenate([weight * jnp.cos(phase), -weight * jnp.sin(phase)], axis=0)


def latitude_tables(lat_ids, total_lat, degree_ids):
    odd_rows = 2 * lat_ids[:, None] + 1
    period = 4 * total_lat
    scale = jnp.pi / (2.0 * total_lat)
    even_arg = (odd_rows * degree_ids[None, :] % period).astype(jnp.float32) * scale
    odd_arg = (odd_rows * (degree_ids[None, :] + 1) % period).astype(jnp.float32) * scale
    return (jnp.cos(even_arg), jnp.sin(odd_arg))


def latitude_forward(waves, even_tab, odd_tab):
    cols, nf, levs, lats = waves.shape
    pairs = waves.reshape(cols // 2, 2, nf, levs, lats)
    even_part = jnp.einsum("pfli,ik->pflk", pairs[:, 0], even_tab, precision=highest)
    odd_part = jnp.einsum("pfli,ik->pflk", pairs[:, 1], odd_tab, precision=highest)
    return jnp.stack([even_part, odd_part], axis=1).reshape(cols, nf, levs, even_tab.shape[1])


def latitude_inverse(spectra, even_tab, odd_tab):
    cols, nf, levs, degs = spectra.shape
    pairs = spectra.reshape(cols // 2, 2, nf, levs, degs)
    even_part = jnp.einsum("pflk,ik->pfli", pairs[:, 0], even_tab, precision=highest)
    odd_part = jnp.einsum("pflk,ik->pfli", pairs[:, 1], odd_tab, precision=highest)
    return jnp.stack([even_part, odd_part], axis=1).reshape(cols, nf, levs, even_tab.shape[0])


def operator(spectra, coeffs, col_waves, degree_ids):
    parity = col_waves % 2
    freq = (degree_ids[None, :] + parity[:, None]).astype(jnp.float32)
    wavenum = col_waves.astype(jnp.float32)[:, None]
    qvalue = ((wavenum * wavenum + freq * freq) / (KMAX * KMAX))[:, None, :]
    hyper = coeffs[0][None, :, None]
    coupling = coeffs[1][None, :, None]
    depth = coeffs[2][None, :, None]
    vort = spectra[:, 0]
    diverg = spectra[:, 1]
    temper = spectra[:, 2]
    new_vort = vort / (1.0 + hyper * qvalue * qvalue)
    new_div = (diverg + coupling * qvalue * temper) / (1.0 + coupling * depth * qvalue)
    new_temp = temper - depth * new_div
    return jnp.stack([new_vort - vort, new_div - diverg, new_temp - temper], axis=1)


def nonlinear(state):
    temper = state[2] + 0.25 * state[0] * state[1]
    return jnp.stack([state[0], state[1], temper], axis=0)


def transposing(fields, spectral_coeffs, mlp_in, mlp_mid, mlp_out):
    nf, lev_dev, lon_dev, lat_dev = fields.shape
    lon_count = lax.axis_size("lon")
    lat_count = lax.axis_size("lat")
    total_lon = lon_dev * lon_count
    total_lat = lat_dev * lat_count
    wave_cols = 2 * WAVES // lon_count
    row_count = nf * lev_dev * lat_dev
    lat_ids = lax.axis_index("lat") * lat_dev + jnp.arange(lat_dev, dtype=jnp.int32)
    col_waves = (lax.axis_index("lon") * wave_cols + jnp.arange(wave_cols, dtype=jnp.int32)) % WAVES
    weight = 2.0 / total_lat
    all_lons = jnp.arange(total_lon, dtype=jnp.int32)
    fwd_full = forward_table(all_lons, total_lon, WAVES)
    inv_full = inverse_table(all_lons, total_lon, WAVES)
    own_degrees = jnp.arange(KMAX, dtype=jnp.int32)
    full_even, full_odd = latitude_tables(lat_ids, total_lat, own_degrees)
    state = fields
    for _ in range(SUBSTEPS):
        flat = state.transpose(0, 1, 3, 2).reshape(row_count, lon_dev)
        by_row = lax.all_to_all(flat, "lon", split_axis=0, concat_axis=1, tiled=True)
        row_waves = jnp.dot(by_row, fwd_full, precision=highest)
        by_col = lax.all_to_all(row_waves, "lon", split_axis=1, concat_axis=0, tiled=True)
        waves = by_col.reshape(nf, lev_dev, lat_dev, wave_cols).transpose(3, 0, 1, 2)
        partial_spectra = latitude_forward(waves, full_even * weight, full_odd * weight)
        spectra = lax.psum(partial_spectra, "lat")
        change = operator(spectra, spectral_coeffs, col_waves, own_degrees)
        back = latitude_inverse(change, full_even, full_odd)
        flat_back = back.transpose(1, 2, 3, 0).reshape(row_count, wave_cols)
        full_waves = lax.all_to_all(flat_back, "lon", split_axis=0, concat_axis=1, tiled=True)
        row_grid = jnp.dot(full_waves, inv_full, precision=highest)
        own_grid = lax.all_to_all(row_grid, "lon", split_axis=1, concat_axis=0, tiled=True)
        increment = own_grid.reshape(nf, lev_dev, lat_dev, lon_dev).transpose(0, 1, 3, 2)
        state = nonlinear(state + increment)
    features = state.astype(jnp.bfloat16).reshape(nf, lev_dev, lon_dev * lat_dev)
    columns = lax.all_to_all(features, "lev", split_axis=2, concat_axis=1, tiled=True)
    levels = columns.shape[1]
    inputs = columns.reshape(nf * levels, columns.shape[2])
    hidden = jax.nn.silu(jnp.dot(mlp_in, inputs, preferred_element_type=jnp.float32)).astype(
        jnp.bfloat16
    )
    hidden = jax.nn.silu(jnp.dot(mlp_mid[0], hidden, preferred_element_type=jnp.float32)).astype(
        jnp.bfloat16
    )
    hidden = jax.nn.silu(jnp.dot(mlp_mid[1], hidden, preferred_element_type=jnp.float32)).astype(
        jnp.bfloat16
    )
    output = jnp.dot(mlp_out, hidden, preferred_element_type=jnp.float32).astype(jnp.bfloat16)
    output = output.reshape(nf, levels, columns.shape[2])
    returned = lax.all_to_all(output, "lev", split_axis=1, concat_axis=2, tiled=True)
    return state + returned.astype(jnp.float32).reshape(state.shape)


class Plan:
    def __init__(self, mesh_shape, local):
        self.nf, self.levs, self.lon_dev, self.lat_dev = local
        self.lons = mesh_shape["lon"]
        self.lats = mesh_shape["lat"]
        self.zs = mesh_shape["lev"]
        self.n_lon = self.lons * self.lon_dev
        self.n_lat = self.lats * self.lat_dev
        self.jpad = round_up(self.lon_dev, 16)
        self.rows = self.lons * self.jpad
        classes = min(self.n_lon // 2 + 1, WAVES)
        self.half = round_up((classes + 1) // 2, 16)
        self.block = 2 * self.half
        self.modes = 2 * self.block
        self.degs = round_up(-(-KMAX // 2), 16)
        self.side = self.lats // 2
        self.feats = round_up(self.nf * self.levs, 8)

    def fits(self):
        plane = self.nf * self.levs * self.n_lon * self.n_lat * 4
        power_of_two = all(n & (n - 1) == 0 for n in (self.lons, self.lats, self.zs))
        return (
            SUBSTEPS == 2
            and self.nf == 3
            and power_of_two
            and plane <= PLANE_LIMIT
            and self.n_lon % 2 == 0
            and self.lats % 2 == 0
            and self.lat_dev == LANES
            and KMAX < self.n_lat
        )


def split_np(table):
    high = table.astype(np.float32).astype(jnp.bfloat16)
    low = (table - high.astype(np.float64)).astype(jnp.bfloat16)
    return high, low


def zonal_tables(plan):
    lon = np.arange(plan.n_lon)
    pos = (lon // plan.lon_dev) * plan.jpad + lon % plan.lon_dev
    scale = 2.0 / (plan.n_lon * plan.n_lat)
    ana = np.zeros((plan.modes, plan.rows))
    syn = np.zeros((plan.rows, plan.modes))
    classes = min(plan.n_lon // 2 + 1, WAVES)
    for rho in range(classes):
        phase = 2.0 * np.pi * ((rho * lon) % plan.n_lon) / plan.n_lon
        cos_row = (rho % 2) * plan.block + rho // 2
        ana[cos_row, pos] = scale * np.cos(phase)
        syn[pos, cos_row] = np.cos(phase)
        if rho > 0 and 2 * rho != plan.n_lon:
            ana[cos_row + plan.half, pos] = -scale * np.sin(phase)
            syn[pos, cos_row + plan.half] = -np.sin(phase)
    ana_h, ana_l = split_np(ana)
    syn_h, syn_l = split_np(syn)
    return (
        np.concatenate([ana_h, ana_l, ana_h], axis=1),
        np.concatenate([syn_h, syn_l, syn_h], axis=1),
    )


def meridional_tables(plan):
    lat = np.arange(plan.n_lat // 2)[None, :]
    deg = np.arange(KMAX)[:, None]
    period = 4 * plan.n_lat
    scale = np.pi / (2.0 * plan.n_lat)
    even = np.cos(((2 * lat + 1) * deg % period) * scale)
    odd = np.sin(((2 * lat + 1) * (deg + 1) % period) * scale)
    out = np.zeros((2, 2, 2, plan.degs, plan.n_lat // 2), dtype=jnp.bfloat16)
    for parity, table in enumerate((even, odd)):
        for kind in range(2):
            for part, value in enumerate(split_np(table[kind::2])):
                out[parity, kind, part, : value.shape[0]] = value
    return out


def split(value):
    high = value.astype(jnp.bfloat16)
    low = (value - high.astype(jnp.float32)).astype(jnp.bfloat16)
    return high, low


def mm(left, right):
    return lax.dot_general(
        left, right, (((1,), (0,)), ((), ())), preferred_element_type=jnp.float32
    )


def mm_l(left, right):
    return lax.dot_general(
        left, right, (((0,), (0,)), ((), ())), preferred_element_type=jnp.float32
    )


def mm_t(left, right):
    return lax.dot_general(
        left, right, (((1,), (1,)), ((), ())), preferred_element_type=jnp.float32
    )


def prepare_kernel(plan, coef_hbm, *refs):
    sources, refs = refs[:3], refs[3:]
    sv_ref, sq_ref, count_ref, gb_ref = refs[:4]
    targets, (coef_ref, sems) = refs[4:7], refs[7:]
    first = pltpu.make_async_copy(coef_hbm, coef_ref, sems.at[3])
    first.start()
    copies = [pltpu.make_async_copy(source, target, sems.at[n]) for n, (source, target) in enumerate(zip(sources, targets))]
    for copy in copies:
        copy.start()
    first.wait()
    for lev in range(plan.levs):
        gb_ref[lev] = jnp.full(gb_ref.shape[1:], coef_ref[lev, 2], jnp.float32)
    row = lax.broadcasted_iota(jnp.int32, (plan.half, plan.degs), 0)
    lane = lax.broadcasted_iota(jnp.int32, (plan.half, plan.degs), 1)
    inv_k2 = 1.0 / (KMAX * KMAX)
    turns = -(-WAVES // plan.n_lon)
    for parity in range(2):
        rho = 2 * row + parity
        terms = []
        for turn in range(turns):
            wave = rho + plan.n_lon * turn
            terms.append((wave, (wave < WAVES) & (2 * rho <= plan.n_lon)))
            wave = plan.n_lon * (turn + 1) - rho
            terms.append((wave, (wave < WAVES) & (rho > 0) & (2 * rho < plan.n_lon)))
        terms = [
            (wave.astype(jnp.float32), jnp.where(valid, jnp.where(wave == 0, 1.0, 2.0), 0.0)) for wave, valid in terms
        ]
        count_ref[parity] = sum(weight for _, weight in terms)
        for kind in range(2):
            freq = (2 * lane + kind + parity).astype(jnp.float32)
            freq2 = freq * freq
            sums = [[jnp.zeros((plan.half, plan.degs), jnp.float32) for _ in range(2)] for _ in range(plan.levs)]
            for wave, weight in terms:
                q = (wave * wave + freq2) * inv_k2
                for lev in range(plan.levs):
                    nu, ga, gb = (coef_ref[lev, i] for i in range(3))
                    hyper = nu * q * q
                    wave_q = ga * q
                    sums[lev][0] -= weight * (hyper / (1.0 + hyper))
                    sums[lev][1] += weight * (wave_q / (1.0 + gb * wave_q))
            for lev in range(plan.levs):
                sv_ref[lev, parity, kind] = sums[lev][0]
                sq_ref[lev, parity, kind] = sums[lev][1]
    for copy in copies:
        copy.wait()


def prepare(plan, coeffs):
    table = jax.ShapeDtypeStruct((plan.levs, 2, 2, plan.half, plan.degs), jnp.float32)
    vmem = pl.BlockSpec(memory_space=pltpu.VMEM)
    tables = [jnp.asarray(t) for t in (*zonal_tables(plan), meridional_tables(plan))]
    out = pl.pallas_call(
        functools.partial(prepare_kernel, plan),
        out_shape=(
            table,
            table,
            jax.ShapeDtypeStruct((2, plan.half, plan.degs), jnp.float32),
            jax.ShapeDtypeStruct((plan.levs, 8, LANES), jnp.float32),
            *(jax.ShapeDtypeStruct(t.shape, t.dtype) for t in tables),
        ),
        in_specs=[pl.BlockSpec(memory_space=pltpu.HBM)] * (1 + len(tables)),
        out_specs=(vmem,) * (4 + len(tables)),
        scratch_shapes=[pltpu.SMEM(coeffs.shape, jnp.float32), pltpu.SemaphoreType.DMA((1 + len(tables),))],
        compiler_params=pltpu.CompilerParams(vmem_limit_bytes=16 * 1024 * 1024),
        name="prepare",
    )(*[pltpu.with_memory_space_constraint(t, pltpu.HBM) for t in (coeffs, *tables)])
    return out[:4], out[4:]


def weights_kernel(plan, win_ref, mid_ref, wout_ref, w1_ref, half_ref, wo_ref):
    half_ref[...] = (0.5 * mid_ref[...].astype(jnp.float32)).astype(jnp.bfloat16)
    own_z = lax.axis_index("lev")
    total = plan.zs * plan.levs
    nin = plan.nf * total

    def feature_of(slot, count):
        block = slot // count
        inner = slot % count
        field = inner // plan.levs
        level = (own_z ^ block) * plan.levs + inner % plan.levs
        return jnp.where(inner < plan.nf * plan.levs, field * total + level, -1)

    count = plan.nf * plan.levs
    wide = plan.zs * count
    source = lax.broadcasted_iota(jnp.int32, (nin, wide), 0)
    slot = lax.broadcasted_iota(jnp.int32, (nin, wide), 1)
    pick = (source == feature_of(slot, count)).astype(jnp.float32).astype(jnp.bfloat16)
    w1_ref[...] = (0.5 * mm_l(win_ref[...], pick)).astype(jnp.bfloat16)
    slot = lax.broadcasted_iota(jnp.int32, (plan.feats, nin), 0)
    source = lax.broadcasted_iota(jnp.int32, (plan.feats, nin), 1)
    pick = (source == feature_of(slot, plan.feats)).astype(jnp.float32).astype(jnp.bfloat16)
    wo_ref[...] = mm(pick, wout_ref[...]).astype(jnp.bfloat16)


def order_weights(plan, mlp_in, mlp_mid, mlp_out):
    units = mlp_in.shape[1]
    vmem = pl.BlockSpec(memory_space=pltpu.VMEM)
    return pl.pallas_call(
        functools.partial(weights_kernel, plan),
        out_shape=(
            jax.ShapeDtypeStruct((units, plan.zs * plan.nf * plan.levs), jnp.bfloat16),
            jax.ShapeDtypeStruct(mlp_mid.shape, jnp.bfloat16),
            jax.ShapeDtypeStruct((plan.feats, units), jnp.bfloat16),
        ),
        in_specs=[vmem] * 3,
        out_specs=(vmem,) * 3,
        compiler_params=pltpu.CompilerParams(vmem_limit_bytes=16 * 1024 * 1024),
        name="order_weights",
    )(mlp_in, mlp_mid, mlp_out)


def dynamics_kernel(plan, blocks, *refs):
    block_refs = refs[:blocks]
    ana_ref, syn_ref, mer_ref, sv_ref, sq_ref, count_ref, gb_ref = refs[blocks : 7 + blocks]
    state_ref, feat_ref = refs[7 + blocks : 9 + blocks]
    grid_ref, prod_ref = refs[9 + blocks :]
    own_lon, own_lat = lax.axis_index("lon"), lax.axis_index("lat")
    nf, levs, lats = plan.nf, plan.levs, plan.lats
    block, half = plan.block, plan.half
    if plan.jpad != plan.lon_dev:
        tail = (plan.lon_dev // 8) * 8
        for lon in range(plan.lons):
            start = lon * plan.jpad + tail
            stop = (lon + 1) * plan.jpad
            zeros = jnp.zeros((stop - start, plan.lat_dev), jnp.float32)
            for side in range(2):
                for lat in range(plan.side):
                    for f in range(nf):
                        for l in range(levs):
                            grid_ref[side, lat, f, l, start:stop, :] = zeros

    def place(lat):
        south = lat >= plan.side
        return jnp.where(south, 1, 0), jnp.where(south, lats - 1 - lat, lat)

    def mirror(value, side):
        lane = lax.broadcasted_iota(jnp.int32, value.shape, 1)
        lane = jnp.where(side == 1, plan.lat_dev - 1 - lane, lane)
        return jnp.take_along_axis(value, lane, axis=1, mode="promise_in_bounds")

    for s in range(blocks):
        lon = own_lon ^ (s % plan.lons)
        side, lat = place(own_lat ^ (s // plan.lons))
        row = pl.multiple_of(lon * plan.jpad, 8)
        for f in range(nf):
            for l in range(levs):
                value = block_refs[s][f, :, l, :]
                grid_ref[side, lat, f, l, pl.ds(row, plan.lon_dev), :] = mirror(value, side)

    def whole(ref, side, *index):
        return jnp.concatenate([ref[(side, lat, *index)] for lat in range(plan.side)], axis=1)

    def analyse(values):
        middle = plan.n_lat // 2
        parts = []
        for north, south in values:
            high, low = split(jnp.concatenate([north + south, north - south], axis=1))
            parts.append(split(mm(ana_ref[...], jnp.concatenate([high, high, low], axis=0))))
        out = []
        for parity in range(2):
            kinds = []
            for kind in range(2):
                lanes = slice(kind * middle, (kind + 1) * middle)
                rows = slice(parity * block, (parity + 1) * block)
                high, low = (jnp.concatenate([part[n][rows, lanes] for part in parts], axis=0) for n in range(2))
                thigh, tlow = mer_ref[parity, kind, 0], mer_ref[parity, kind, 1]
                count = high.shape[0]
                tall = mm_t(jnp.concatenate([high, low], axis=0), thigh)
                kinds.append(tall[:count] + tall[count:] + mm_t(high, tlow))
            out.append(kinds)
        return out

    def synthesise(spectra, rows, table):
        parts = []
        for parity in range(2):
            kinds = []
            for kind in range(2):
                high, low = split(spectra[parity][kind])
                thigh, tlow = table(parity, kind)
                size = thigh.shape[1]
                if size <= LANES:
                    wide = mm(high, jnp.concatenate([thigh, tlow], axis=1))
                    kinds.append(wide[:, :size] + wide[:, size:] + mm(low, thigh))
                else:
                    kinds.append(mm(high, thigh) + mm(low, thigh) + mm(high, tlow))
            parts.append(jnp.concatenate(kinds, axis=1))
        count = spectra[0][0].shape[0] // block
        width = parts[0].shape[1] // 2
        out = []
        for n in range(count):
            both = jnp.concatenate([part[n * block : (n + 1) * block] for part in parts], axis=0)
            high, low = split(both)
            grid = mm(rows, jnp.concatenate([high, high, low], axis=0))
            out.append((grid[:, :width], grid[:, width:]))
        return out

    def at(spectrum, f, l):
        n = f * levs + l
        return spectrum[n * block : (n + 1) * block]

    pairs = [(parity, kind) for parity in range(2) for kind in range(2)]
    lane = lax.broadcasted_iota(jnp.int32, (block, plan.degs), 1)
    cls = lax.broadcasted_iota(jnp.int32, (block, plan.degs), 0) % half
    norms, counts = {}, {}
    for parity in range(2):
        rho = 2 * cls + parity
        alone = (rho == 0) | (2 * rho == plan.n_lon)
        norm = jnp.where(alone, 1.0, 0.5)
        weight = jnp.concatenate([count_ref[parity]] * 2, axis=0)
        for kind in range(2):
            counts[parity, kind] = weight
            norms[parity, kind] = norm * jnp.where(lane == 0, 2.0, 1.0) if parity == kind == 0 else norm

    def changes(spectra):
        out = {}
        for pair in pairs:
            per = [[None] * levs for _ in range(nf)]
            for l in range(levs):
                sv = jnp.concatenate([sv_ref[(l, *pair)]] * 2, axis=0)
                sq = jnp.concatenate([sq_ref[(l, *pair)]] * 2, axis=0)
                gb = gb_ref[l, 0:1, 0:1]
                vort, diverg, temper = (spectra[pair][f][l] for f in range(3))
                per[0][l] = sv * vort
                per[1][l] = sq * (temper - gb * diverg)
                per[2][l] = -gb * (counts[pair] * diverg + per[1][l])
            out[pair] = per
        return out

    def stack(nested, fields):
        return [
            [
                jnp.concatenate([nested[parity, kind][f][l] for f in fields for l in range(levs)], axis=0)
                for kind in range(2)
            ]
            for parity in range(2)
        ]

    flat = analyse([tuple(whole(grid_ref, side, f, l) for side in range(2)) for f in range(nf) for l in range(levs)])
    spectra = {
        (parity, kind): [[at(flat[parity][kind], f, l) for l in range(levs)] for f in range(nf)]
        for parity, kind in pairs
    }
    first = changes(spectra)
    grown = synthesise(
        stack(first, (0, 1)), syn_ref[...], lambda parity, kind: (mer_ref[parity, kind, 0], mer_ref[parity, kind, 1])
    )
    products = []
    for l in range(levs):
        (vsym, vanti), (dsym, danti) = grown[l], grown[levs + l]
        sides = []
        for side in range(2):
            vort = whole(grid_ref, side, 0, l) + (vsym - vanti if side else vsym + vanti)
            diverg = whole(grid_ref, side, 1, l) + (dsym - danti if side else dsym + danti)
            product = 0.25 * vort * diverg
            for lat in range(plan.side):
                prod_ref[side, lat, l] = product[:, lat * plan.lat_dev : (lat + 1) * plan.lat_dev]
            sides.append(product)
        products.append(tuple(sides))
    extra = analyse(products)
    updated = {}
    for pair in pairs:
        per = [[spectra[pair][f][l] + norms[pair] * first[pair][f][l] for l in range(levs)] for f in range(nf)]
        per[2] = [per[2][l] + at(extra[pair[0]][pair[1]], 0, l) for l in range(levs)]
        updated[pair] = per
    second = changes(updated)
    both = {
        pair: [[first[pair][f][l] + second[pair][f][l] for l in range(levs)] for f in range(nf)] for pair in pairs
    }
    side, lat = place(own_lat)
    own_start = pl.multiple_of(lat * plan.lat_dev, LANES)
    own_row = pl.multiple_of(own_lon * plan.jpad, 8)
    own = synthesise(
        stack(both, range(nf)),
        syn_ref[pl.ds(own_row, plan.jpad), :],
        lambda parity, kind: tuple(mer_ref[parity, kind, part, :, pl.ds(own_start, plan.lat_dev)] for part in range(2)),
    )
    sign = jnp.where(side == 1, -1.0, 1.0)
    for l in range(levs):
        vort, diverg, temper = (
            grid_ref[side, lat, f, l, pl.ds(own_row, plan.jpad), :]
            + (own[f * levs + l][0] + sign * own[f * levs + l][1])
            for f in range(3)
        )
        temper = temper + prod_ref[side, lat, l, pl.ds(own_row, plan.jpad), :] + 0.25 * vort * diverg
        for f, value in enumerate((vort, diverg, temper)):
            value = mirror(value, side)
            state_ref[f, l] = value[: plan.lon_dev]
            feat_ref[f * levs + l] = value.astype(jnp.bfloat16)


def dynamics(plan, blocks, tables, sums):
    vmem = pl.BlockSpec(memory_space=pltpu.VMEM)
    return pl.pallas_call(
        functools.partial(dynamics_kernel, plan, len(blocks)),
        out_shape=(
            jax.ShapeDtypeStruct((plan.nf, plan.levs, plan.lon_dev, plan.lat_dev), jnp.float32),
            jax.ShapeDtypeStruct((plan.nf * plan.levs, plan.jpad, plan.lat_dev), jnp.bfloat16),
        ),
        in_specs=[vmem] * (len(blocks) + 7),
        out_specs=(vmem,) * 2,
        scratch_shapes=[
            pltpu.VMEM((2, plan.side, plan.nf, plan.levs, plan.rows, plan.lat_dev), jnp.float32),
            pltpu.VMEM((2, plan.side, plan.levs, plan.rows, plan.lat_dev), jnp.float32),
        ],
        compiler_params=pltpu.CompilerParams(vmem_limit_bytes=32 * 1024 * 1024),
        name="dynamics",
    )(*blocks, *tables, *sums)


def silu_of_half(half):
    return (half + half * jnp.tanh(half)).astype(jnp.bfloat16)


def network_kernel(plan, blocks, groups, *refs):
    block_refs = refs[:blocks]
    w1_ref, mid_ref, wo_ref, state_ref, out_ref, wide_ref, tile_ref, sum_ref, sems = refs[blocks:]
    features = plan.nf * plan.levs
    rows = features * plan.jpad
    for s, ref in enumerate(block_refs):
        wide_ref[s * rows : (s + 1) * rows, :] = ref[...].astype(jnp.float32).reshape(rows, plan.lat_dev)
    copies = []
    for number, (start, stop) in enumerate(groups):
        inputs = jnp.concatenate(
            [
                wide_ref[pl.ds(lon, blocks * features, stride=plan.jpad), :].astype(jnp.bfloat16)
                for lon in range(start, stop)
            ],
            axis=1,
        )
        hidden = silu_of_half(mm(w1_ref[...], inputs))
        hidden = silu_of_half(mm(mid_ref[0], hidden))
        hidden = silu_of_half(mm(mid_ref[1], hidden))
        output = mm(wo_ref[...], hidden).astype(jnp.bfloat16).astype(jnp.float32)
        for lon in range(start, stop):
            tile_ref[lon] = output[:, (lon - start) * plan.lat_dev : (lon - start + 1) * plan.lat_dev]
        for f in range(plan.nf):
            for l in range(plan.levs):
                correction = tile_ref[start:stop, f * plan.levs + l, :]
                sum_ref[f, start:stop, l, :] = state_ref[f, l, start:stop, :] + correction
            part = (f, pl.ds(start, stop - start))
            copy = pltpu.make_async_copy(sum_ref.at[part], out_ref.at[part], sems.at[number, f])
            copy.start()
            copies.append(copy)
    for copy in copies:
        copy.wait()


def network(plan, state, blocks, weights):
    vmem = pl.BlockSpec(memory_space=pltpu.VMEM)
    size = max(1, GROUP // plan.lat_dev)
    groups = [(start, min(start + size, plan.lon_dev)) for start in range(0, plan.lon_dev, size)]
    out = jax.ShapeDtypeStruct((plan.nf, plan.lon_dev, plan.levs, plan.lat_dev), jnp.float32)
    return pl.pallas_call(
        functools.partial(network_kernel, plan, len(blocks), groups),
        out_shape=out,
        in_specs=[vmem] * (len(blocks) + 4),
        out_specs=pl.BlockSpec(memory_space=pltpu.HBM),
        scratch_shapes=[
            pltpu.VMEM((len(blocks) * plan.nf * plan.levs * plan.jpad, plan.lat_dev), jnp.float32),
            pltpu.VMEM((plan.lon_dev, plan.feats, plan.lat_dev), jnp.float32),
            pltpu.VMEM(out.shape, jnp.float32),
            pltpu.SemaphoreType.DMA((len(groups), plan.nf)),
        ],
        compiler_params=pltpu.CompilerParams(vmem_limit_bytes=24 * 1024 * 1024),
        name="network",
    )(*blocks, *weights, state)


def swap(value, axes, sizes, mask):
    count = int(np.prod(sizes))
    return lax.ppermute(value, axes, [(i, i ^ mask) for i in range(count)])


def gathering(plan, fields, spectral_coeffs, mlp_in, mlp_mid, mlp_out):
    fields = fields.transpose(0, 2, 1, 3)
    plane = ("lon", "lat")
    sizes = (plan.lons, plan.lats)
    blocks = [None] * (plan.lons * plan.lats)
    outer = [(lon, lat) for lat in range(0, plan.lats, 2) for lon in range(plan.lons)]
    for lon, lat in outer:
        mask = lon * plan.lats + lat
        blocks[lat * plan.lons + lon] = swap(fields, plane, sizes, mask) if mask else fields
    if plan.lats > 1:
        for lon, lat in outer:
            blocks[(lat ^ 1) * plan.lons + lon] = swap(blocks[lat * plan.lons + lon], plane, sizes, 1)
    sums, tables = prepare(plan, spectral_coeffs.T)
    weights = order_weights(plan, mlp_in.T, mlp_mid, mlp_out)
    state, feats = dynamics(plan, blocks, tables, sums)
    parts = [feats]
    for mask in range(1, plan.zs):
        parts.append(swap(feats, ("lev",), (plan.zs,), mask))
    return network(plan, state, parts, weights).transpose(0, 2, 1, 3)


def solution(mesh):
    in_specs = (P(None, "lev", "lon", "lat"), P(None, "lev"), P(), P(), P())
    out_specs = P(None, "lev", "lon", "lat")

    def per_device(fields, spectral_coeffs, mlp_in, mlp_mid, mlp_out):
        plan = Plan(mesh.shape, fields.shape)
        if plan.fits():
            return gathering(plan, fields, spectral_coeffs, mlp_in, mlp_mid, mlp_out)
        return transposing(fields, spectral_coeffs, mlp_in, mlp_mid, mlp_out)

    def step(fields, *rest):
        return jax.shard_map(
            per_device, mesh=mesh, in_specs=in_specs, out_specs=out_specs, check_vma=False
        )(fields, *rest)

    return step
```

profile of v0, /device:TPU:0, one launch (start us, length us, event | category | flops | bytes accessed | tf_op | source)
XLA Modules:
  0.0 30.0 jit_solution(3427987714016575235)
XLA Ops:
  0.0 3.0 %collective-permute-start = (f32[3,30,2,128]{3,2,1,0:T(2,128)}, f32[3,30,2,128]{3,2,1,0:T(2,128)S(1)}, u32[]{:S(2)}, u32[]{:S(2)}) collective-permute-start(f32[3,30,2,128]{3,2,1,0:T(2,128)} %bitcast.4), channel_id=1, source_target_pairs={{0,16},{4,20},{8,24},{12,28},{16,0},{20,4},{24,8},{28,12},{1,17},{... | collective-permute-start | bytes 276488 | tf_op jit(solution)/shard_map/ppermute | solution.py:614
  3.0 1.5 %collective-permute-start.3 = (f32[3,30,2,128]{3,2,1,0:T(2,128)}, f32[3,30,2,128]{3,2,1,0:T(2,128)S(1)}, u32[]{:S(2)}, u32[]{:S(2)}) collective-permute-start(f32[3,30,2,128]{3,2,1,0:T(2,128)} %bitcast.5), channel_id=1, source_target_pairs={{0,8},{4,12},{8,0},{12,4},{16,24},{20,28},{24,16},{28,20},{1,9},{5... | collective-permute-start | bytes 276488 | tf_op jit(solution)/shard_map/ppermute | solution.py:614
  4.5 0.0 collective-permute-start.4
  4.5 0.0 collective-permute-start.1
  4.5 1.7 %collective-permute-done.refs_1_ = f32[3,30,2,128]{3,2,1,0:T(2,128)S(1)} collective-permute-done((f32[3,30,2,128]{3,2,1,0:T(2,128)}, f32[3,30,2,128]{3,2,1,0:T(2,128)S(1)}, u32[]{:S(2)}, u32[]{:S(2)}) %collective-permute-start) | collective-permute-done | bytes 92192 | tf_op jit(solution)/shard_map/ppermute | solution.py:614
  6.2 0.0 collective-permute-start.2
  6.2 2.5 %collective-permute-done.3.refs_4_ = f32[3,30,2,128]{3,2,1,0:T(2,128)S(1)} collective-permute-done((f32[3,30,2,128]{3,2,1,0:T(2,128)}, f32[3,30,2,128]{3,2,1,0:T(2,128)S(1)}, u32[]{:S(2)}, u32[]{:S(2)}) %collective-permute-start.3) | collective-permute-done | bytes 92192 | tf_op jit(solution)/shard_map/ppermute | solution.py:614
  8.7 0.0 collective-permute-start.5
  8.7 1.4 %collective-permute-done.4.refs_5_ = f32[3,30,2,128]{3,2,1,0:T(2,128)S(1)} collective-permute-done((f32[3,30,2,128]{3,2,1,0:T(2,128)}, f32[3,30,2,128]{3,2,1,0:T(2,128)S(1)}, u32[]{:S(2)}, u32[]{:S(2)}) %collective-permute-start.4) | collective-permute-done | bytes 92192 | tf_op jit(solution)/shard_map/ppermute | solution.py:614
  10.2 1.8 %prepare.1 = (f32[2,2,2,16,160]{4,3,2,1,0:T(8,128)S(1)}, f32[2,2,2,16,160]{4,3,2,1,0:T(8,128)S(1)}, f32[2,16,160]{2,1,0:T(8,128)S(1)}, f32[2,8,128]{2,1,0:T(8,12...) custom-call(f32[2,3]{1,0:T(2,128)} %bitcast.10, ...), custom_call_target="tpu_custom_call" | custom-call | tf_op jit(solution)/shard_map/prepare/pallas_call | solution.py:295
  12.0 0.0 collective-permute-done.1.refs_2_
  12.0 0.0 collective-permute-done.2.refs_3_
  12.0 0.0 copy-start
  12.0 0.0 copy-start.2
  12.0 0.0 copy-start.3
  12.1 2.8 %dynamics.1 = (f32[3,2,30,128]{3,2,1,0:T(8,128)S(1)}, bf16[6,32,128]{2,1,0:T(8,128)(2,1)S(1)}) custom-call(f32[3,30,2,128]{3,2,1,0:T(2,128)S(1)} %bitcast.8, f32[3,30,2,128]{3,2,1,0:T(2,128)S(1)} %collective-permute-done.refs_1_, f32[3,30,2,128]{3,2,1,0:T(2,128)S(1)} %collective-permute-done.1.refs_2_, f32[3,30,2,128]{3,2,1,0:T(2,128)S(1)} %collective-permute-done.2.refs_3_, ...), custom_call_target="tpu_custom_call" | custom-call | tf_op jit(solution)/shard_map/dynamics/pallas_call | solution.py:536
  14.8 1.6 %collective-permute-start.7 = (bf16[6,32,128]{2,1,0:T(8,128)(2,1)S(1)}, bf16[6,32,128]{2,1,0:T(8,128)(2,1)S(1)}, u32[]{:S(2)}, u32[]{:S(2)}) collective-permute-start(bf16[6,32,128]{2,1,0:T(8,128)(2,1)S(1)} %get-tuple-element.24.refs_0_), channel_id=1, source_target_pairs={{0,1},{1,0},{2,3},{3,2},{4,5},{5,4},{6,7},{7,6},{8,9},{9,8},{10,11... | collective-permute-start | bytes 147464 | tf_op jit(solution)/shard_map/ppermute | solution.py:614
  16.4 2.6 %collective-permute-start.8 = (bf16[6,32,128]{2,1,0:T(8,128)(2,1)S(1)}, bf16[6,32,128]{2,1,0:T(8,128)(2,1)S(1)}, u32[]{:S(2)}, u32[]{:S(2)}) collective-permute-start(bf16[6,32,128]{2,1,0:T(8,128)(2,1)S(1)} %get-tuple-element.24.refs_0_), channel_id=1, source_target_pairs={{0,2},{1,3},{2,0},{3,1},{4,6},{5,7},{6,4},{7,5},{8,10},{9,11},{10,... | collective-permute-start | bytes 147464 | tf_op jit(solution)/shard_map/ppermute | solution.py:614
  19.0 0.3 collective-permute-start.9
  19.3 0.4 %order_weights.1 = (bf16[384,24]{1,0:T(8,128)(2,1)S(1)}, bf16[2,384,384]{2,1,0:T(8,128)(2,1)S(1)}, bf16[8,384]{1,0:T(8,128)(2,1)S(1)}) custom-call(bf16[24,384]{1,0:T(8,128)(2,1)S(1)} %bitcast.9, bf16[2,384,384]{2,1,0:T(8,128)(2,1)S(1)} %copy-done, bf16[24,384]{1,0:T(8,128)(2,1)S(1)} %copy-done.3), custom_call_target="tpu_custom_call" | custom-call | tf_op jit(solution)/shard_map/order_weights/pallas_call | solution.py:341
  19.7 0.0 collective-permute-done.7.refs_1_
  19.7 2.9 %collective-permute-done.8.refs_2_ = bf16[6,32,128]{2,1,0:T(8,128)(2,1)S(1)} collective-permute-done((bf16[6,32,128]{2,1,0:T(8,128)(2,1)S(1)}, bf16[6,32,128]{2,1,0:T(8,128)(2,1)S(1)}, u32[]{:S(2)}, u32[]{:S(2)}) %collective-permute-start.8) | collective-permute-done | bytes 49184 | tf_op jit(solution)/shard_map/ppermute | solution.py:614
  22.6 2.3 %collective-permute-done.9.refs_3_ = bf16[6,32,128]{2,1,0:T(8,128)(2,1)S(1)} collective-permute-done((bf16[6,32,128]{2,1,0:T(8,128)(2,1)S(1)}, bf16[6,32,128]{2,1,0:T(8,128)(2,1)S(1)}, u32[]{:S(2)}, u32[]{:S(2)}) %collective-permute-start.9) | collective-permute-done | bytes 49184 | tf_op jit(solution)/shard_map/ppermute | solution.py:614
  24.9 5.1 %network.1 = f32[3,30,2,128]{3,2,1,0:T(2,128)} custom-call(bf16[6,32,128]{2,1,0:T(8,128)(2,1)S(1)} %get-tuple-element.24.refs_0_, bf16[6,32,128]{2,1,0:T(8,128)(2,1)S(1)} %collective-permute-done.7.refs_1_, bf16[6,32,128]{2,1,0:T(8,128)(2,1)S(1)} %collective-permute-done.8.refs_2_, bf16[6,32,128]{2,1,0:T(8,128)(2,1)S(1)} %collective-permute-done.9.refs_3_, ...), custom_call_target="tpu_custom_call" | custom-call | tf_op jit(solution)/shard_map/network/pallas_call | solution.py:596
  (8 shorter events, 0.0 us)
Async XLA Ops:
  0.0 6.2 %collective-permute-start = (f32[3,30,2,128]{3,2,1,0:T(2,128)}, f32[3,30,2,128]{3,2,1,0:T(2,128)S(1)}, u32[]{:S(2)}, u32[]{:S(2)}) collective-permute-start(f32[3,30,2,128]{3,2,1,0:T(2,128)} %bitcast.4), channel_id=1, source_target_pairs={{0,16},{4,20},{8,24},{12,28},{16,0},{20,4},{24,8},{28,12},{1,17},{... | collective-permute-start | bytes 276488 | tf_op jit(solution)/shard_map/ppermute | solution.py:614
  3.0 5.7 %collective-permute-start.3 = (f32[3,30,2,128]{3,2,1,0:T(2,128)}, f32[3,30,2,128]{3,2,1,0:T(2,128)S(1)}, u32[]{:S(2)}, u32[]{:S(2)}) collective-permute-start(f32[3,30,2,128]{3,2,1,0:T(2,128)} %bitcast.5), channel_id=1, source_target_pairs={{0,8},{4,12},{8,0},{12,4},{16,24},{20,28},{24,16},{28,20},{1,9},{5... | collective-permute-start | bytes 276488 | tf_op jit(solution)/shard_map/ppermute | solution.py:614
  4.5 5.7 %collective-permute-start.4 = (f32[3,30,2,128]{3,2,1,0:T(2,128)}, f32[3,30,2,128]{3,2,1,0:T(2,128)S(1)}, u32[]{:S(2)}, u32[]{:S(2)}) collective-permute-start(f32[3,30,2,128]{3,2,1,0:T(2,128)} %bitcast.6), channel_id=1, source_target_pairs={{0,24},{4,28},{8,16},{12,20},{16,8},{20,12},{24,0},{28,4},{1,25},{... | collective-permute-start | bytes 276488 | tf_op jit(solution)/shard_map/ppermute | solution.py:614
  4.5 7.5 %collective-permute-start.1 = (f32[3,30,2,128]{3,2,1,0:T(2,128)}, f32[3,30,2,128]{3,2,1,0:T(2,128)S(1)}, u32[]{:S(2)}, u32[]{:S(2)}) collective-permute-start(f32[3,30,2,128]{3,2,1,0:T(2,128)} %bitcast.7), channel_id=1, source_target_pairs={{0,4},{4,0},{8,12},{12,8},{16,20},{20,16},{24,28},{28,24},{1,5},{5... | collective-permute-start | bytes 276488 | tf_op jit(solution)/shard_map/ppermute | solution.py:614
  6.2 5.8 %collective-permute-start.2 = (f32[3,30,2,128]{3,2,1,0:T(2,128)S(1)}, f32[3,30,2,128]{3,2,1,0:T(2,128)S(1)}, u32[]{:S(2)}, u32[]{:S(2)}) collective-permute-start(f32[3,30,2,128]{3,2,1,0:T(2,128)S(1)} %collective-permute-done.refs_1_), channel_id=1, source_target_pairs={{0,4},{4,0},{8,12},{12,8},{16,20},{20,16},{24,28},{28,24},{1,5},{5... | collective-permute-start | bytes 276488 | tf_op jit(solution)/shard_map/ppermute | solution.py:614
  8.7 3.3 %collective-permute-start.5 = (f32[3,30,2,128]{3,2,1,0:T(2,128)S(1)}, f32[3,30,2,128]{3,2,1,0:T(2,128)S(1)}, u32[]{:S(2)}, u32[]{:S(2)}) collective-permute-start(f32[3,30,2,128]{3,2,1,0:T(2,128)S(1)} %collective-permute-done.3.refs_4_), channel_id=1, source_target_pairs={{0,4},{4,0},{8,12},{12,8},{16,20},{20,16},{24,28},{28,24},{1,5},{5... | collective-permute-start | bytes 276488 | tf_op jit(solution)/shard_map/ppermute | solution.py:614
  10.1 1.9 %collective-permute-start.6 = (f32[3,30,2,128]{3,2,1,0:T(2,128)S(1)}, f32[3,30,2,128]{3,2,1,0:T(2,128)S(1)}, u32[]{:S(2)}, u32[]{:S(2)}) collective-permute-start(f32[3,30,2,128]{3,2,1,0:T(2,128)S(1)} %collective-permute-done.4.refs_5_), channel_id=1, source_target_pairs={{0,4},{4,0},{8,12},{12,8},{16,20},{20,16},{24,28},{28,24},{1,5},{5... | collective-permute-start | bytes 276488 | tf_op jit(solution)/shard_map/ppermute | solution.py:614
  10.2 1.9 %copy-start.1 = (f32[3,2,30,128]{3,1,2,0:T(2,128)S(1)}, f32[3,2,30,128]{3,1,2,0:T(2,128)}, u32[]{:S(2)}) copy-start(f32[3,2,30,128]{3,1,2,0:T(2,128)} %param.8) | copy-start | bytes 276484
  12.0 7.3 %copy-start = (bf16[2,384,384]{2,1,0:T(8,128)(2,1)S(1)}, bf16[2,384,384]{2,1,0:T(8,128)(2,1)}, u32[]{:S(2)}) copy-start(bf16[2,384,384]{2,1,0:T(8,128)(2,1)} %mid_ref.1) | copy-start | bytes 1769476
  12.0 7.2 %copy-start.2 = (bf16[384,24]{0,1:T(8,128)(2,1)S(1)}, bf16[384,24]{0,1:T(8,128)(2,1)}, u32[]{:S(2)}) copy-start(bf16[384,24]{0,1:T(8,128)(2,1)} %param.10) | copy-start | bytes 55300
  12.0 7.2 %copy-start.3 = (bf16[24,384]{1,0:T(8,128)(2,1)S(1)}, bf16[24,384]{1,0:T(8,128)(2,1)}, u32[]{:S(2)}) copy-start(bf16[24,384]{1,0:T(8,128)(2,1)} %wout_ref.1) | copy-start | bytes 55300
  14.8 4.8 %collective-permute-start.7 = (bf16[6,32,128]{2,1,0:T(8,128)(2,1)S(1)}, bf16[6,32,128]{2,1,0:T(8,128)(2,1)S(1)}, u32[]{:S(2)}, u32[]{:S(2)}) collective-permute-start(bf16[6,32,128]{2,1,0:T(8,128)(2,1)S(1)} %get-tuple-element.24.refs_0_), channel_id=1, source_target_pairs={{0,1},{1,0},{2,3},{3,2},{4,5},{5,4},{6,7},{7,6},{8,9},{9,8},{10,11... | collective-permute-start | bytes 147464 | tf_op jit(solution)/shard_map/ppermute | solution.py:614
  16.4 6.1 %collective-permute-start.8 = (bf16[6,32,128]{2,1,0:T(8,128)(2,1)S(1)}, bf16[6,32,128]{2,1,0:T(8,128)(2,1)S(1)}, u32[]{:S(2)}, u32[]{:S(2)}) collective-permute-start(bf16[6,32,128]{2,1,0:T(8,128)(2,1)S(1)} %get-tuple-element.24.refs_0_), channel_id=1, source_target_pairs={{0,2},{1,3},{2,0},{3,1},{4,6},{5,7},{6,4},{7,5},{8,10},{9,11},{10,... | collective-permute-start | bytes 147464 | tf_op jit(solution)/shard_map/ppermute | solution.py:614
  19.0 5.9 %collective-permute-start.9 = (bf16[6,32,128]{2,1,0:T(8,128)(2,1)S(1)}, bf16[6,32,128]{2,1,0:T(8,128)(2,1)S(1)}, u32[]{:S(2)}, u32[]{:S(2)}) collective-permute-start(bf16[6,32,128]{2,1,0:T(8,128)(2,1)S(1)} %get-tuple-element.24.refs_0_), channel_id=1, source_target_pairs={{0,3},{1,2},{2,1},{3,0},{4,7},{5,6},{6,5},{7,4},{8,11},{9,10},{10,... | collective-permute-start | bytes 147464 | tf_op jit(solution)/shard_map/ppermute | solution.py:614
where the time goes:
time: 30.2 us; the launch traced here: 30 us
  waiting for transfers between devices  10.9 us (36%)
  Pallas kernels  10.1 us (33%)
  starting transfers between devices  8.95 us (30%)
    ppermute x10, waiting for transfers between devices, swap(): return lax.ppermute(value, axes, [(i, i ^ mask) for i in range(count)])  10.9 us
    ppermute x10, starting transfers between devices, swap(): return lax.ppermute(value, axes, [(i, i ^ mask) for i in range(count)])  8.95 us
    pallas_call x1, Pallas kernels, network(): pl.pallas_call(functools.partial(network_kernel, plan, len(blocks), group...  5.12 us
    pallas_call x1, Pallas kernels, dynamics(): pl.pallas_call(functools.partial(dynamics_kernel, plan, len(blocks)), out...  2.75 us
    pallas_call x1, Pallas kernels, prepare(): pl.pallas_call(functools.partial(prepare_kernel, plan), out_shape=(table,...  1.8 us
  transfers between devices with their start and end apart: 10, of which 5 were waited for; matrix products, arithmetic and copies ran while one was open for 0% of the time, Pallas kernels for 7%

commit v1 on v0

--- a/solution.py
+++ b/solution.py
@@ -356,7 +356,7 @@
     block_refs = refs[:blocks]
     ana_ref, syn_ref, mer_ref, sv_ref, sq_ref, count_ref, gb_ref = refs[blocks : 7 + blocks]
     state_ref, feat_ref = refs[7 + blocks : 9 + blocks]
-    grid_ref, prod_ref = refs[9 + blocks :]
+    grid_ref, prod_ref, pack_ref = refs[9 + blocks :]
     own_lon, own_lat = lax.axis_index("lon"), lax.axis_index("lat")
     nf, levs, lats = plan.nf, plan.levs, plan.lats
     block, half = plan.block, plan.half
@@ -528,7 +528,9 @@
         for f, value in enumerate((vort, diverg, temper)):
             value = mirror(value, side)
             state_ref[f, l] = value[: plan.lon_dev]
-            feat_ref[f * levs + l] = value.astype(jnp.bfloat16)
+            start = (f * levs + l) * plan.lon_dev
+            pack_ref[start : start + plan.lon_dev, :] = value[: plan.lon_dev]
+    feat_ref[...] = pack_ref[: feat_ref.shape[0], :].astype(jnp.bfloat16)
 
 
 def dynamics(plan, blocks, tables, sums):
@@ -537,13 +539,14 @@
         functools.partial(dynamics_kernel, plan, len(blocks)),
         out_shape=(
             jax.ShapeDtypeStruct((plan.nf, plan.levs, plan.lon_dev, plan.lat_dev), jnp.float32),
-            jax.ShapeDtypeStruct((plan.nf * plan.levs, plan.jpad, plan.lat_dev), jnp.bfloat16),
+            jax.ShapeDtypeStruct((plan.nf * plan.levs * plan.lon_dev, plan.lat_dev), jnp.bfloat16),
         ),
         in_specs=[vmem] * (len(blocks) + 7),
         out_specs=(vmem,) * 2,
         scratch_shapes=[
             pltpu.VMEM((2, plan.side, plan.nf, plan.levs, plan.rows, plan.lat_dev), jnp.float32),
             pltpu.VMEM((2, plan.side, plan.levs, plan.rows, plan.lat_dev), jnp.float32),
+            pltpu.VMEM((round_up(plan.nf * plan.levs * plan.lon_dev, 8) + 8, plan.lat_dev), jnp.float32),
         ],
         compiler_params=pltpu.CompilerParams(vmem_limit_bytes=32 * 1024 * 1024),
         name="dynamics",
@@ -558,14 +561,14 @@
     block_refs = refs[:blocks]
     w1_ref, mid_ref, wo_ref, state_ref, out_ref, wide_ref, tile_ref, sum_ref, sems = refs[blocks:]
     features = plan.nf * plan.levs
-    rows = features * plan.jpad
+    rows = features * plan.lon_dev
     for s, ref in enumerate(block_refs):
-        wide_ref[s * rows : (s + 1) * rows, :] = ref[...].astype(jnp.float32).reshape(rows, plan.lat_dev)
+        wide_ref[s * rows : (s + 1) * rows, :] = ref[...].astype(jnp.float32)
     copies = []
     for number, (start, stop) in enumerate(groups):
         inputs = jnp.concatenate(
             [
-                wide_ref[pl.ds(lon, blocks * features, stride=plan.jpad), :].astype(jnp.bfloat16)
+                wide_ref[pl.ds(lon, blocks * features, stride=plan.lon_dev), :].astype(jnp.bfloat16)
                 for lon in range(start, stop)
             ],
             axis=1,
@@ -599,7 +602,7 @@
         in_specs=[vmem] * (len(blocks) + 4),
         out_specs=pl.BlockSpec(memory_space=pltpu.HBM),
         scratch_shapes=[
-            pltpu.VMEM((len(blocks) * plan.nf * plan.levs * plan.jpad, plan.lat_dev), jnp.float32),
+            pltpu.VMEM((round_up(len(blocks) * plan.nf * plan.levs * plan.lon_dev, 8) + 8, plan.lat_dev), jnp.float32),
             pltpu.VMEM((plan.lon_dev, plan.feats, plan.lat_dev), jnp.float32),
             pltpu.VMEM(out.shape, jnp.float32),
             pltpu.SemaphoreType.DMA((len(groups), plan.nf)),

time: 30.2 us -> 30.1 us (level)
  no operation moved by 1% of the time
where the time goes in v1:
time: 30.1 us; the launch traced here: 30 us
  waiting for transfers between devices  10.9 us (36%)
  Pallas kernels  10 us (33%)
  starting transfers between devices  8.95 us (30%)
    ppermute x10, waiting for transfers between devices, swap(): return lax.ppermute(value, axes, [(i, i ^ mask) for i in range(count)])  10.9 us
    ppermute x10, starting transfers between devices, swap(): return lax.ppermute(value, axes, [(i, i ^ mask) for i in range(count)])  8.95 us
    pallas_call x1, Pallas kernels, network(): pl.pallas_call(functools.partial(network_kernel, plan, len(blocks), group...  5.09 us
    pallas_call x1, Pallas kernels, dynamics(): pl.pallas_call(functools.partial(dynamics_kernel, plan, len(blocks)), out...  2.76 us
    pallas_call x1, Pallas kernels, prepare(): pl.pallas_call(functools.partial(prepare_kernel, plan), out_shape=(table,...  1.8 us
  transfers between devices with their start and end apart: 10, of which 5 were waited for; matrix products, arithmetic and copies ran while one was open for 0% of the time, Pallas kernels for 7%

profile of v1, /device:TPU:0, one launch (start us, length us, event | category | flops | bytes accessed | tf_op | source)
XLA Modules:
  0.0 30.0 jit_solution(9829907470626848196)
XLA Ops:
  0.0 3.0 %collective-permute-start = (f32[3,30,2,128]{3,2,1,0:T(2,128)}, f32[3,30,2,128]{3,2,1,0:T(2,128)S(1)}, u32[]{:S(2)}, u32[]{:S(2)}) collective-permute-start(f32[3,30,2,128]{3,2,1,0:T(2,128)} %bitcast.4), channel_id=1, source_target_pairs={{0,16},{4,20},{8,24},{12,28},{16,0},{20,4},{24,8},{28,12},{1,17},{... | collective-permute-start | bytes 276488 | tf_op jit(solution)/shard_map/ppermute | solution.py:617
  3.0 1.5 %collective-permute-start.3 = (f32[3,30,2,128]{3,2,1,0:T(2,128)}, f32[3,30,2,128]{3,2,1,0:T(2,128)S(1)}, u32[]{:S(2)}, u32[]{:S(2)}) collective-permute-start(f32[3,30,2,128]{3,2,1,0:T(2,128)} %bitcast.5), channel_id=1, source_target_pairs={{0,8},{4,12},{8,0},{12,4},{16,24},{20,28},{24,16},{28,20},{1,9},{5... | collective-permute-start | bytes 276488 | tf_op jit(solution)/shard_map/ppermute | solution.py:617
  4.5 0.0 collective-permute-start.4
  4.5 0.0 collective-permute-start.1
  4.5 1.7 %collective-permute-done.refs_1_ = f32[3,30,2,128]{3,2,1,0:T(2,128)S(1)} collective-permute-done((f32[3,30,2,128]{3,2,1,0:T(2,128)}, f32[3,30,2,128]{3,2,1,0:T(2,128)S(1)}, u32[]{:S(2)}, u32[]{:S(2)}) %collective-permute-start) | collective-permute-done | bytes 92192 | tf_op jit(solution)/shard_map/ppermute | solution.py:617
  6.2 0.0 collective-permute-start.2
  6.2 2.5 %collective-permute-done.3.refs_4_ = f32[3,30,2,128]{3,2,1,0:T(2,128)S(1)} collective-permute-done((f32[3,30,2,128]{3,2,1,0:T(2,128)}, f32[3,30,2,128]{3,2,1,0:T(2,128)S(1)}, u32[]{:S(2)}, u32[]{:S(2)}) %collective-permute-start.3) | collective-permute-done | bytes 92192 | tf_op jit(solution)/shard_map/ppermute | solution.py:617
  8.7 0.0 collective-permute-start.5
  8.7 1.4 %collective-permute-done.4.refs_5_ = f32[3,30,2,128]{3,2,1,0:T(2,128)S(1)} collective-permute-done((f32[3,30,2,128]{3,2,1,0:T(2,128)}, f32[3,30,2,128]{3,2,1,0:T(2,128)S(1)}, u32[]{:S(2)}, u32[]{:S(2)}) %collective-permute-start.4) | collective-permute-done | bytes 92192 | tf_op jit(solution)/shard_map/ppermute | solution.py:617
  10.2 1.8 %prepare.1 = (f32[2,2,2,16,160]{4,3,2,1,0:T(8,128)S(1)}, f32[2,2,2,16,160]{4,3,2,1,0:T(8,128)S(1)}, f32[2,16,160]{2,1,0:T(8,128)S(1)}, f32[2,8,128]{2,1,0:T(8,12...) custom-call(f32[2,3]{1,0:T(2,128)} %bitcast.10, ...), custom_call_target="tpu_custom_call" | custom-call | tf_op jit(solution)/shard_map/prepare/pallas_call | solution.py:295
  12.0 0.0 collective-permute-done.1.refs_2_
  12.0 0.0 collective-permute-done.2.refs_3_
  12.0 0.0 copy-start
  12.0 0.0 copy-start.2
  12.0 0.0 copy-start.3
  12.1 2.8 %dynamics.1 = (f32[3,2,30,128]{3,2,1,0:T(8,128)S(1)}, bf16[180,128]{1,0:T(8,128)(2,1)S(1)}) custom-call(f32[3,30,2,128]{3,2,1,0:T(2,128)S(1)} %bitcast.8, f32[3,30,2,128]{3,2,1,0:T(2,128)S(1)} %collective-permute-done.refs_1_, f32[3,30,2,128]{3,2,1,0:T(2,128)S(1)} %collective-permute-done.1.refs_2_, f32[3,30,2,128]{3,2,1,0:T(2,128)S(1)} %collective-permute-done.2.refs_3_, ...), custom_call_target="tpu_custom_call" | custom-call | tf_op jit(solution)/shard_map/dynamics/pallas_call | solution.py:538
  14.8 1.6 %collective-permute-start.7 = (bf16[180,128]{1,0:T(8,128)(2,1)S(1)}, bf16[180,128]{1,0:T(8,128)(2,1)S(1)}, u32[]{:S(2)}, u32[]{:S(2)}) collective-permute-start(bf16[180,128]{1,0:T(8,128)(2,1)S(1)} %get-tuple-element.24.refs_0_), channel_id=1, source_target_pairs={{0,1},{1,0},{2,3},{3,2},{4,5},{5,4},{6,7},{7,6},{8,9},{9,8},{10,11... | collective-permute-start | bytes 138248 | tf_op jit(solution)/shard_map/ppermute | solution.py:617
  16.4 2.6 %collective-permute-start.8 = (bf16[180,128]{1,0:T(8,128)(2,1)S(1)}, bf16[180,128]{1,0:T(8,128)(2,1)S(1)}, u32[]{:S(2)}, u32[]{:S(2)}) collective-permute-start(bf16[180,128]{1,0:T(8,128)(2,1)S(1)} %get-tuple-element.24.refs_0_), channel_id=1, source_target_pairs={{0,2},{1,3},{2,0},{3,1},{4,6},{5,7},{6,4},{7,5},{8,10},{9,11},{10,... | collective-permute-start | bytes 138248 | tf_op jit(solution)/shard_map/ppermute | solution.py:617
  19.0 0.3 collective-permute-start.9
  19.3 0.4 %order_weights.1 = (bf16[384,24]{1,0:T(8,128)(2,1)S(1)}, bf16[2,384,384]{2,1,0:T(8,128)(2,1)S(1)}, bf16[8,384]{1,0:T(8,128)(2,1)S(1)}) custom-call(bf16[24,384]{1,0:T(8,128)(2,1)S(1)} %bitcast.9, bf16[2,384,384]{2,1,0:T(8,128)(2,1)S(1)} %copy-done, bf16[24,384]{1,0:T(8,128)(2,1)S(1)} %copy-done.3), custom_call_target="tpu_custom_call" | custom-call | tf_op jit(solution)/shard_map/order_weights/pallas_call | solution.py:341
  19.7 0.0 collective-permute-done.7.refs_1_
  19.7 2.8 %collective-permute-done.8.refs_2_ = bf16[180,128]{1,0:T(8,128)(2,1)S(1)} collective-permute-done((bf16[180,128]{1,0:T(8,128)(2,1)S(1)}, bf16[180,128]{1,0:T(8,128)(2,1)S(1)}, u32[]{:S(2)}, u32[]{:S(2)}) %collective-permute-start.8) | collective-permute-done | bytes 46112 | tf_op jit(solution)/shard_map/ppermute | solution.py:617
  22.5 2.4 %collective-permute-done.9.refs_3_ = bf16[180,128]{1,0:T(8,128)(2,1)S(1)} collective-permute-done((bf16[180,128]{1,0:T(8,128)(2,1)S(1)}, bf16[180,128]{1,0:T(8,128)(2,1)S(1)}, u32[]{:S(2)}, u32[]{:S(2)}) %collective-permute-start.9) | collective-permute-done | bytes 46112 | tf_op jit(solution)/shard_map/ppermute | solution.py:617
  24.9 5.1 %network.1 = f32[3,30,2,128]{3,2,1,0:T(2,128)} custom-call(bf16[180,128]{1,0:T(8,128)(2,1)S(1)} %get-tuple-element.24.refs_0_, bf16[180,128]{1,0:T(8,128)(2,1)S(1)} %collective-permute-done.7.refs_1_, bf16[180,128]{1,0:T(8,128)(2,1)S(1)} %collective-permute-done.8.refs_2_, bf16[180,128]{1,0:T(8,128)(2,1)S(1)} %collective-permute-done.9.refs_3_, ...), custom_call_target="tpu_custom_call" | custom-call | tf_op jit(solution)/shard_map/network/pallas_call | solution.py:599
  (8 shorter events, 0.0 us)
Async XLA Ops:
  0.0 6.2 %collective-permute-start = (f32[3,30,2,128]{3,2,1,0:T(2,128)}, f32[3,30,2,128]{3,2,1,0:T(2,128)S(1)}, u32[]{:S(2)}, u32[]{:S(2)}) collective-permute-start(f32[3,30,2,128]{3,2,1,0:T(2,128)} %bitcast.4), channel_id=1, source_target_pairs={{0,16},{4,20},{8,24},{12,28},{16,0},{20,4},{24,8},{28,12},{1,17},{... | collective-permute-start | bytes 276488 | tf_op jit(solution)/shard_map/ppermute | solution.py:617
  3.0 5.7 %collective-permute-start.3 = (f32[3,30,2,128]{3,2,1,0:T(2,128)}, f32[3,30,2,128]{3,2,1,0:T(2,128)S(1)}, u32[]{:S(2)}, u32[]{:S(2)}) collective-permute-start(f32[3,30,2,128]{3,2,1,0:T(2,128)} %bitcast.5), channel_id=1, source_target_pairs={{0,8},{4,12},{8,0},{12,4},{16,24},{20,28},{24,16},{28,20},{1,9},{5... | collective-permute-start | bytes 276488 | tf_op jit(solution)/shard_map/ppermute | solution.py:617
  4.5 5.7 %collective-permute-start.4 = (f32[3,30,2,128]{3,2,1,0:T(2,128)}, f32[3,30,2,128]{3,2,1,0:T(2,128)S(1)}, u32[]{:S(2)}, u32[]{:S(2)}) collective-permute-start(f32[3,30,2,128]{3,2,1,0:T(2,128)} %bitcast.6), channel_id=1, source_target_pairs={{0,24},{4,28},{8,16},{12,20},{16,8},{20,12},{24,0},{28,4},{1,25},{... | collective-permute-start | bytes 276488 | tf_op jit(solution)/shard_map/ppermute | solution.py:617
  4.5 7.5 %collective-permute-start.1 = (f32[3,30,2,128]{3,2,1,0:T(2,128)}, f32[3,30,2,128]{3,2,1,0:T(2,128)S(1)}, u32[]{:S(2)}, u32[]{:S(2)}) collective-permute-start(f32[3,30,2,128]{3,2,1,0:T(2,128)} %bitcast.7), channel_id=1, source_target_pairs={{0,4},{4,0},{8,12},{12,8},{16,20},{20,16},{24,28},{28,24},{1,5},{5... | collective-permute-start | bytes 276488 | tf_op jit(solution)/shard_map/ppermute | solution.py:617
  6.2 5.8 %collective-permute-start.2 = (f32[3,30,2,128]{3,2,1,0:T(2,128)S(1)}, f32[3,30,2,128]{3,2,1,0:T(2,128)S(1)}, u32[]{:S(2)}, u32[]{:S(2)}) collective-permute-start(f32[3,30,2,128]{3,2,1,0:T(2,128)S(1)} %collective-permute-done.refs_1_), channel_id=1, source_target_pairs={{0,4},{4,0},{8,12},{12,8},{16,20},{20,16},{24,28},{28,24},{1,5},{5... | collective-permute-start | bytes 276488 | tf_op jit(solution)/shard_map/ppermute | solution.py:617
  8.7 3.3 %collective-permute-start.5 = (f32[3,30,2,128]{3,2,1,0:T(2,128)S(1)}, f32[3,30,2,128]{3,2,1,0:T(2,128)S(1)}, u32[]{:S(2)}, u32[]{:S(2)}) collective-permute-start(f32[3,30,2,128]{3,2,1,0:T(2,128)S(1)} %collective-permute-done.3.refs_4_), channel_id=1, source_target_pairs={{0,4},{4,0},{8,12},{12,8},{16,20},{20,16},{24,28},{28,24},{1,5},{5... | collective-permute-start | bytes 276488 | tf_op jit(solution)/shard_map/ppermute | solution.py:617
  10.1 1.9 %collective-permute-start.6 = (f32[3,30,2,128]{3,2,1,0:T(2,128)S(1)}, f32[3,30,2,128]{3,2,1,0:T(2,128)S(1)}, u32[]{:S(2)}, u32[]{:S(2)}) collective-permute-start(f32[3,30,2,128]{3,2,1,0:T(2,128)S(1)} %collective-permute-done.4.refs_5_), channel_id=1, source_target_pairs={{0,4},{4,0},{8,12},{12,8},{16,20},{20,16},{24,28},{28,24},{1,5},{5... | collective-permute-start | bytes 276488 | tf_op jit(solution)/shard_map/ppermute | solution.py:617
  10.2 1.9 %copy-start.1 = (f32[3,2,30,128]{3,1,2,0:T(2,128)S(1)}, f32[3,2,30,128]{3,1,2,0:T(2,128)}, u32[]{:S(2)}) copy-start(f32[3,2,30,128]{3,1,2,0:T(2,128)} %param.8) | copy-start | bytes 276484
  12.0 7.3 %copy-start = (bf16[2,384,384]{2,1,0:T(8,128)(2,1)S(1)}, bf16[2,384,384]{2,1,0:T(8,128)(2,1)}, u32[]{:S(2)}) copy-start(bf16[2,384,384]{2,1,0:T(8,128)(2,1)} %mid_ref.1) | copy-start | bytes 1769476
  12.0 7.2 %copy-start.2 = (bf16[384,24]{0,1:T(8,128)(2,1)S(1)}, bf16[384,24]{0,1:T(8,128)(2,1)}, u32[]{:S(2)}) copy-start(bf16[384,24]{0,1:T(8,128)(2,1)} %param.10) | copy-start | bytes 55300
  12.0 7.2 %copy-start.3 = (bf16[24,384]{1,0:T(8,128)(2,1)S(1)}, bf16[24,384]{1,0:T(8,128)(2,1)}, u32[]{:S(2)}) copy-start(bf16[24,384]{1,0:T(8,128)(2,1)} %wout_ref.1) | copy-start | bytes 55300
  14.8 4.8 %collective-permute-start.7 = (bf16[180,128]{1,0:T(8,128)(2,1)S(1)}, bf16[180,128]{1,0:T(8,128)(2,1)S(1)}, u32[]{:S(2)}, u32[]{:S(2)}) collective-permute-start(bf16[180,128]{1,0:T(8,128)(2,1)S(1)} %get-tuple-element.24.refs_0_), channel_id=1, source_target_pairs={{0,1},{1,0},{2,3},{3,2},{4,5},{5,4},{6,7},{7,6},{8,9},{9,8},{10,11... | collective-permute-start | bytes 138248 | tf_op jit(solution)/shard_map/ppermute | solution.py:617
  16.4 6.0 %collective-permute-start.8 = (bf16[180,128]{1,0:T(8,128)(2,1)S(1)}, bf16[180,128]{1,0:T(8,128)(2,1)S(1)}, u32[]{:S(2)}, u32[]{:S(2)}) collective-permute-start(bf16[180,128]{1,0:T(8,128)(2,1)S(1)} %get-tuple-element.24.refs_0_), channel_id=1, source_target_pairs={{0,2},{1,3},{2,0},{3,1},{4,6},{5,7},{6,4},{7,5},{8,10},{9,11},{10,... | collective-permute-start | bytes 138248 | tf_op jit(solution)/shard_map/ppermute | solution.py:617
  19.0 5.9 %collective-permute-start.9 = (bf16[180,128]{1,0:T(8,128)(2,1)S(1)}, bf16[180,128]{1,0:T(8,128)(2,1)S(1)}, u32[]{:S(2)}, u32[]{:S(2)}) collective-permute-start(bf16[180,128]{1,0:T(8,128)(2,1)S(1)} %get-tuple-element.24.refs_0_), channel_id=1, source_target_pairs={{0,3},{1,2},{2,1},{3,0},{4,7},{5,6},{6,5},{7,4},{8,11},{9,10},{10,... | collective-permute-start | bytes 138248 | tf_op jit(solution)/shard_map/ppermute | solution.py:617

commit v2 on v1

--- a/solution.py
+++ b/solution.py
@@ -583,10 +583,10 @@
             for l in range(plan.levs):
                 correction = tile_ref[start:stop, f * plan.levs + l, :]
                 sum_ref[f, start:stop, l, :] = state_ref[f, l, start:stop, :] + correction
-            part = (f, pl.ds(start, stop - start))
-            copy = pltpu.make_async_copy(sum_ref.at[part], out_ref.at[part], sems.at[number, f])
-            copy.start()
-            copies.append(copy)
+        part = (slice(None), pl.ds(start, stop - start))
+        copy = pltpu.make_async_copy(sum_ref.at[part], out_ref.at[part], sems.at[number])
+        copy.start()
+        copies.append(copy)
     for copy in copies:
         copy.wait()
 
@@ -605,7 +605,7 @@
             pltpu.VMEM((round_up(len(blocks) * plan.nf * plan.levs * plan.lon_dev, 8) + 8, plan.lat_dev), jnp.float32),
             pltpu.VMEM((plan.lon_dev, plan.feats, plan.lat_dev), jnp.float32),
             pltpu.VMEM(out.shape, jnp.float32),
-            pltpu.SemaphoreType.DMA((len(groups), plan.nf)),
+            pltpu.SemaphoreType.DMA((len(groups),)),
         ],
         compiler_params=pltpu.CompilerParams(vmem_limit_bytes=24 * 1024 * 1024),
         name="network",

time: 30.1 us -> 30.1 us (level)
  no operation moved by 1% of the time
where the time goes in v2:
time: 30.1 us; the launch traced here: 29.9 us
  waiting for transfers between devices  10.9 us (36%)
  Pallas kernels  9.97 us (33%)
  starting transfers between devices  8.95 us (30%)
    ppermute x10, waiting for transfers between devices, swap(): return lax.ppermute(value, axes, [(i, i ^ mask) for i in range(count)])  10.9 us
    ppermute x10, starting transfers between devices, swap(): return lax.ppermute(value, axes, [(i, i ^ mask) for i in range(count)])  8.95 us
    pallas_call x1, Pallas kernels, network(): pl.pallas_call(functools.partial(network_kernel, plan, len(blocks), group...  5.03 us
    pallas_call x1, Pallas kernels, dynamics(): pl.pallas_call(functools.partial(dynamics_kernel, plan, len(blocks)), out...  2.76 us
    pallas_call x1, Pallas kernels, prepare(): pl.pallas_call(functools.partial(prepare_kernel, plan), out_shape=(table,...  1.8 us
  transfers between devices with their start and end apart: 10, of which 5 were waited for; matrix products, arithmetic and copies ran while one was open for 0% of the time, Pallas kernels for 7%

profile of v2, /device:TPU:0, one launch (start us, length us, event | category | flops | bytes accessed | tf_op | source)
XLA Modules:
  0.0 29.9 jit_solution(7006359241891229598)
XLA Ops:
  0.0 3.0 %collective-permute-start = (f32[3,30,2,128]{3,2,1,0:T(2,128)}, f32[3,30,2,128]{3,2,1,0:T(2,128)S(1)}, u32[]{:S(2)}, u32[]{:S(2)}) collective-permute-start(f32[3,30,2,128]{3,2,1,0:T(2,128)} %bitcast.4), channel_id=1, source_target_pairs={{0,16},{4,20},{8,24},{12,28},{16,0},{20,4},{24,8},{28,12},{1,17},{... | collective-permute-start | bytes 276488 | tf_op jit(solution)/shard_map/ppermute | solution.py:617
  3.0 1.5 %collective-permute-start.3 = (f32[3,30,2,128]{3,2,1,0:T(2,128)}, f32[3,30,2,128]{3,2,1,0:T(2,128)S(1)}, u32[]{:S(2)}, u32[]{:S(2)}) collective-permute-start(f32[3,30,2,128]{3,2,1,0:T(2,128)} %bitcast.5), channel_id=1, source_target_pairs={{0,8},{4,12},{8,0},{12,4},{16,24},{20,28},{24,16},{28,20},{1,9},{5... | collective-permute-start | bytes 276488 | tf_op jit(solution)/shard_map/ppermute | solution.py:617
  4.5 0.0 collective-permute-start.4
  4.5 0.0 collective-permute-start.1
  4.5 1.7 %collective-permute-done.refs_1_ = f32[3,30,2,128]{3,2,1,0:T(2,128)S(1)} collective-permute-done((f32[3,30,2,128]{3,2,1,0:T(2,128)}, f32[3,30,2,128]{3,2,1,0:T(2,128)S(1)}, u32[]{:S(2)}, u32[]{:S(2)}) %collective-permute-start) | collective-permute-done | bytes 92192 | tf_op jit(solution)/shard_map/ppermute | solution.py:617
  6.2 0.0 collective-permute-start.2
  6.2 2.5 %collective-permute-done.3.refs_4_ = f32[3,30,2,128]{3,2,1,0:T(2,128)S(1)} collective-permute-done((f32[3,30,2,128]{3,2,1,0:T(2,128)}, f32[3,30,2,128]{3,2,1,0:T(2,128)S(1)}, u32[]{:S(2)}, u32[]{:S(2)}) %collective-permute-start.3) | collective-permute-done | bytes 92192 | tf_op jit(solution)/shard_map/ppermute | solution.py:617
  8.7 0.0 collective-permute-start.5
  8.7 1.4 %collective-permute-done.4.refs_5_ = f32[3,30,2,128]{3,2,1,0:T(2,128)S(1)} collective-permute-done((f32[3,30,2,128]{3,2,1,0:T(2,128)}, f32[3,30,2,128]{3,2,1,0:T(2,128)S(1)}, u32[]{:S(2)}, u32[]{:S(2)}) %collective-permute-start.4) | collective-permute-done | bytes 92192 | tf_op jit(solution)/shard_map/ppermute | solution.py:617
  10.2 1.8 %prepare.1 = (f32[2,2,2,16,160]{4,3,2,1,0:T(8,128)S(1)}, f32[2,2,2,16,160]{4,3,2,1,0:T(8,128)S(1)}, f32[2,16,160]{2,1,0:T(8,128)S(1)}, f32[2,8,128]{2,1,0:T(8,12...) custom-call(f32[2,3]{1,0:T(2,128)} %bitcast.10, ...), custom_call_target="tpu_custom_call" | custom-call | tf_op jit(solution)/shard_map/prepare/pallas_call | solution.py:295
  12.0 0.0 collective-permute-done.1.refs_2_
  12.0 0.0 collective-permute-done.2.refs_3_
  12.0 0.0 copy-start
  12.0 0.0 copy-start.2
  12.0 0.0 copy-start.3
  12.1 2.8 %dynamics.1 = (f32[3,2,30,128]{3,2,1,0:T(8,128)S(1)}, bf16[180,128]{1,0:T(8,128)(2,1)S(1)}) custom-call(f32[3,30,2,128]{3,2,1,0:T(2,128)S(1)} %bitcast.8, f32[3,30,2,128]{3,2,1,0:T(2,128)S(1)} %collective-permute-done.refs_1_, f32[3,30,2,128]{3,2,1,0:T(2,128)S(1)} %collective-permute-done.1.refs_2_, f32[3,30,2,128]{3,2,1,0:T(2,128)S(1)} %collective-permute-done.2.refs_3_, ...), custom_call_target="tpu_custom_call" | custom-call | tf_op jit(solution)/shard_map/dynamics/pallas_call | solution.py:538
  14.8 1.6 %collective-permute-start.7 = (bf16[180,128]{1,0:T(8,128)(2,1)S(1)}, bf16[180,128]{1,0:T(8,128)(2,1)S(1)}, u32[]{:S(2)}, u32[]{:S(2)}) collective-permute-start(bf16[180,128]{1,0:T(8,128)(2,1)S(1)} %get-tuple-element.24.refs_0_), channel_id=1, source_target_pairs={{0,1},{1,0},{2,3},{3,2},{4,5},{5,4},{6,7},{7,6},{8,9},{9,8},{10,11... | collective-permute-start | bytes 138248 | tf_op jit(solution)/shard_map/ppermute | solution.py:617
  16.4 2.6 %collective-permute-start.8 = (bf16[180,128]{1,0:T(8,128)(2,1)S(1)}, bf16[180,128]{1,0:T(8,128)(2,1)S(1)}, u32[]{:S(2)}, u32[]{:S(2)}) collective-permute-start(bf16[180,128]{1,0:T(8,128)(2,1)S(1)} %get-tuple-element.24.refs_0_), channel_id=1, source_target_pairs={{0,2},{1,3},{2,0},{3,1},{4,6},{5,7},{6,4},{7,5},{8,10},{9,11},{10,... | collective-permute-start | bytes 138248 | tf_op jit(solution)/shard_map/ppermute | solution.py:617
  19.0 0.3 collective-permute-start.9
  19.3 0.4 %order_weights.1 = (bf16[384,24]{1,0:T(8,128)(2,1)S(1)}, bf16[2,384,384]{2,1,0:T(8,128)(2,1)S(1)}, bf16[8,384]{1,0:T(8,128)(2,1)S(1)}) custom-call(bf16[24,384]{1,0:T(8,128)(2,1)S(1)} %bitcast.9, bf16[2,384,384]{2,1,0:T(8,128)(2,1)S(1)} %copy-done, bf16[24,384]{1,0:T(8,128)(2,1)S(1)} %copy-done.3), custom_call_target="tpu_custom_call" | custom-call | tf_op jit(solution)/shard_map/order_weights/pallas_call | solution.py:341
  19.7 0.0 collective-permute-done.7.refs_1_
  19.7 2.8 %collective-permute-done.8.refs_2_ = bf16[180,128]{1,0:T(8,128)(2,1)S(1)} collective-permute-done((bf16[180,128]{1,0:T(8,128)(2,1)S(1)}, bf16[180,128]{1,0:T(8,128)(2,1)S(1)}, u32[]{:S(2)}, u32[]{:S(2)}) %collective-permute-start.8) | collective-permute-done | bytes 46112 | tf_op jit(solution)/shard_map/ppermute | solution.py:617
  22.5 2.4 %collective-permute-done.9.refs_3_ = bf16[180,128]{1,0:T(8,128)(2,1)S(1)} collective-permute-done((bf16[180,128]{1,0:T(8,128)(2,1)S(1)}, bf16[180,128]{1,0:T(8,128)(2,1)S(1)}, u32[]{:S(2)}, u32[]{:S(2)}) %collective-permute-start.9) | collective-permute-done | bytes 46112 | tf_op jit(solution)/shard_map/ppermute | solution.py:617
  24.9 5.0 %network.1 = f32[3,30,2,128]{3,2,1,0:T(2,128)} custom-call(bf16[180,128]{1,0:T(8,128)(2,1)S(1)} %get-tuple-element.24.refs_0_, bf16[180,128]{1,0:T(8,128)(2,1)S(1)} %collective-permute-done.7.refs_1_, bf16[180,128]{1,0:T(8,128)(2,1)S(1)} %collective-permute-done.8.refs_2_, bf16[180,128]{1,0:T(8,128)(2,1)S(1)} %collective-permute-done.9.refs_3_, ...), custom_call_target="tpu_custom_call" | custom-call | tf_op jit(solution)/shard_map/network/pallas_call | solution.py:599
  (8 shorter events, 0.0 us)
Async XLA Ops:
  0.0 6.2 %collective-permute-start = (f32[3,30,2,128]{3,2,1,0:T(2,128)}, f32[3,30,2,128]{3,2,1,0:T(2,128)S(1)}, u32[]{:S(2)}, u32[]{:S(2)}) collective-permute-start(f32[3,30,2,128]{3,2,1,0:T(2,128)} %bitcast.4), channel_id=1, source_target_pairs={{0,16},{4,20},{8,24},{12,28},{16,0},{20,4},{24,8},{28,12},{1,17},{... | collective-permute-start | bytes 276488 | tf_op jit(solution)/shard_map/ppermute | solution.py:617
  3.0 5.7 %collective-permute-start.3 = (f32[3,30,2,128]{3,2,1,0:T(2,128)}, f32[3,30,2,128]{3,2,1,0:T(2,128)S(1)}, u32[]{:S(2)}, u32[]{:S(2)}) collective-permute-start(f32[3,30,2,128]{3,2,1,0:T(2,128)} %bitcast.5), channel_id=1, source_target_pairs={{0,8},{4,12},{8,0},{12,4},{16,24},{20,28},{24,16},{28,20},{1,9},{5... | collective-permute-start | bytes 276488 | tf_op jit(solution)/shard_map/ppermute | solution.py:617
  4.5 5.7 %collective-permute-start.4 = (f32[3,30,2,128]{3,2,1,0:T(2,128)}, f32[3,30,2,128]{3,2,1,0:T(2,128)S(1)}, u32[]{:S(2)}, u32[]{:S(2)}) collective-permute-start(f32[3,30,2,128]{3,2,1,0:T(2,128)} %bitcast.6), channel_id=1, source_target_pairs={{0,24},{4,28},{8,16},{12,20},{16,8},{20,12},{24,0},{28,4},{1,25},{... | collective-permute-start | bytes 276488 | tf_op jit(solution)/shard_map/ppermute | solution.py:617
  4.5 7.5 %collective-permute-start.1 = (f32[3,30,2,128]{3,2,1,0:T(2,128)}, f32[3,30,2,128]{3,2,1,0:T(2,128)S(1)}, u32[]{:S(2)}, u32[]{:S(2)}) collective-permute-start(f32[3,30,2,128]{3,2,1,0:T(2,128)} %bitcast.7), channel_id=1, source_target_pairs={{0,4},{4,0},{8,12},{12,8},{16,20},{20,16},{24,28},{28,24},{1,5},{5... | collective-permute-start | bytes 276488 | tf_op jit(solution)/shard_map/ppermute | solution.py:617
  6.2 5.8 %collective-permute-start.2 = (f32[3,30,2,128]{3,2,1,0:T(2,128)S(1)}, f32[3,30,2,128]{3,2,1,0:T(2,128)S(1)}, u32[]{:S(2)}, u32[]{:S(2)}) collective-permute-start(f32[3,30,2,128]{3,2,1,0:T(2,128)S(1)} %collective-permute-done.refs_1_), channel_id=1, source_target_pairs={{0,4},{4,0},{8,12},{12,8},{16,20},{20,16},{24,28},{28,24},{1,5},{5... | collective-permute-start | bytes 276488 | tf_op jit(solution)/shard_map/ppermute | solution.py:617
  8.7 3.3 %collective-permute-start.5 = (f32[3,30,2,128]{3,2,1,0:T(2,128)S(1)}, f32[3,30,2,128]{3,2,1,0:T(2,128)S(1)}, u32[]{:S(2)}, u32[]{:S(2)}) collective-permute-start(f32[3,30,2,128]{3,2,1,0:T(2,128)S(1)} %collective-permute-done.3.refs_4_), channel_id=1, source_target_pairs={{0,4},{4,0},{8,12},{12,8},{16,20},{20,16},{24,28},{28,24},{1,5},{5... | collective-permute-start | bytes 276488 | tf_op jit(solution)/shard_map/ppermute | solution.py:617
  10.1 1.9 %collective-permute-start.6 = (f32[3,30,2,128]{3,2,1,0:T(2,128)S(1)}, f32[3,30,2,128]{3,2,1,0:T(2,128)S(1)}, u32[]{:S(2)}, u32[]{:S(2)}) collective-permute-start(f32[3,30,2,128]{3,2,1,0:T(2,128)S(1)} %collective-permute-done.4.refs_5_), channel_id=1, source_target_pairs={{0,4},{4,0},{8,12},{12,8},{16,20},{20,16},{24,28},{28,24},{1,5},{5... | collective-permute-start | bytes 276488 | tf_op jit(solution)/shard_map/ppermute | solution.py:617
  10.2 1.9 %copy-start.1 = (f32[3,2,30,128]{3,1,2,0:T(2,128)S(1)}, f32[3,2,30,128]{3,1,2,0:T(2,128)}, u32[]{:S(2)}) copy-start(f32[3,2,30,128]{3,1,2,0:T(2,128)} %param.8) | copy-start | bytes 276484
  12.0 7.3 %copy-start = (bf16[2,384,384]{2,1,0:T(8,128)(2,1)S(1)}, bf16[2,384,384]{2,1,0:T(8,128)(2,1)}, u32[]{:S(2)}) copy-start(bf16[2,384,384]{2,1,0:T(8,128)(2,1)} %mid_ref.1) | copy-start | bytes 1769476
  12.0 7.2 %copy-start.2 = (bf16[384,24]{0,1:T(8,128)(2,1)S(1)}, bf16[384,24]{0,1:T(8,128)(2,1)}, u32[]{:S(2)}) copy-start(bf16[384,24]{0,1:T(8,128)(2,1)} %param.10) | copy-start | bytes 55300
  12.0 7.2 %copy-start.3 = (bf16[24,384]{1,0:T(8,128)(2,1)S(1)}, bf16[24,384]{1,0:T(8,128)(2,1)}, u32[]{:S(2)}) copy-start(bf16[24,384]{1,0:T(8,128)(2,1)} %wout_ref.1) | copy-start | bytes 55300
  14.8 4.8 %collective-permute-start.7 = (bf16[180,128]{1,0:T(8,128)(2,1)S(1)}, bf16[180,128]{1,0:T(8,128)(2,1)S(1)}, u32[]{:S(2)}, u32[]{:S(2)}) collective-permute-start(bf16[180,128]{1,0:T(8,128)(2,1)S(1)} %get-tuple-element.24.refs_0_), channel_id=1, source_target_pairs={{0,1},{1,0},{2,3},{3,2},{4,5},{5,4},{6,7},{7,6},{8,9},{9,8},{10,11... | collective-permute-start | bytes 138248 | tf_op jit(solution)/shard_map/ppermute | solution.py:617
  16.4 6.0 %collective-permute-start.8 = (bf16[180,128]{1,0:T(8,128)(2,1)S(1)}, bf16[180,128]{1,0:T(8,128)(2,1)S(1)}, u32[]{:S(2)}, u32[]{:S(2)}) collective-permute-start(bf16[180,128]{1,0:T(8,128)(2,1)S(1)} %get-tuple-element.24.refs_0_), channel_id=1, source_target_pairs={{0,2},{1,3},{2,0},{3,1},{4,6},{5,7},{6,4},{7,5},{8,10},{9,11},{10,... | collective-permute-start | bytes 138248 | tf_op jit(solution)/shard_map/ppermute | solution.py:617
  19.0 5.9 %collective-permute-start.9 = (bf16[180,128]{1,0:T(8,128)(2,1)S(1)}, bf16[180,128]{1,0:T(8,128)(2,1)S(1)}, u32[]{:S(2)}, u32[]{:S(2)}) collective-permute-start(bf16[180,128]{1,0:T(8,128)(2,1)S(1)} %get-tuple-element.24.refs_0_), channel_id=1, source_target_pairs={{0,3},{1,2},{2,1},{3,0},{4,7},{5,6},{6,5},{7,4},{8,11},{9,10},{10,... | collective-permute-start | bytes 138248 | tf_op jit(solution)/shard_map/ppermute | solution.py:617
